TPU v7x, 32 devices: a whole 2x2x4 slice. The times are simulated.
32 devices in a mesh: groups: 2 (over x), blk: 8 (over z, y), rows: 2 (over core).
Axes of the slice: x: 2, y: 2, z: 4, core: 2. Of those that a mesh axis runs over, the one named last changes fastest.
Arguments:
- queries: bfloat16 [256, 2048], P(('groups', 'blk'), 'rows'), parts along dimension 0, may hold values from -170 to 170
- cache_keys: bfloat16 [8192, 256], P(('groups', 'blk'), 'rows'), parts along dimension 0, may hold values from -6 to 6
- cache_values: bfloat16 [8192, 256], P(('groups', 'blk'), 'rows'), parts along dimension 0, may hold values from -6 to 6
- span_starts: int32 [4], P('groups'), parts along dimension 0, may hold values from 0 to 4032, as said below
- out_weight: bfloat16 [2048, 2048], P(('rows', 'blk')), may hold values from -0.125 to 0.125
- norm_gain: bfloat16 [2048], replicated, may hold values from 0.099609375 to 1.8984375
- expert_ids: int32 [256, 8], P(('groups', 'blk', 'rows')), parts along dimension 0, may hold values from 0 to 15, all different within a row; in each aligned block of 8 rows (0 to 7, 8 to 15, ...) at most 8 rows name the same one
- gate_fixed: int32 [256, 8], P(('groups', 'blk', 'rows')), parts along dimension 0, may hold values from 1 to 4095
- gate_weight: bfloat16 [16, 2048, 768], P(('blk', 'rows')), may hold values from -0.125 to 0.125
- up_weight: bfloat16 [16, 2048, 768], P(('blk', 'rows')), may hold values from -0.125 to 0.125
- down_weight: bfloat16 [16, 768, 2048], P(('blk', 'rows')), may hold values from -0.21875 to 0.21875
Outputs:
- attn_proj: bfloat16 [256, 2048], P(('groups', 'blk', 'rows')), parts along dimension 0
- expert_out: bfloat16 [256, 2048], P(('groups', 'blk', 'rows')), parts along dimension 0
There are 2 independent parts, one for each index of `groups`. A program takes and returns all parts, laid end to end along the dimension named above; an argument that names none is the same for every part. Nothing has to cross between parts.
Inputs may be any that keep to these rules, and one draw needn't show every extreme that they name: `span_starts`: the last span ends at the last cached position, entry 1 is 4032; entry 0 is at most 3968. `expert_ids`: each token names 8 different experts; among the tokens of one device (aligned blocks of 8 rows) no expert is named more than 8 times.
All inputs are finite; a program needn't handle non-finite values.
Results may differ from a plain program's by a relative error of at most 0.035.
Values may be sent and summed in bfloat16 or wider, within the bound.
No kernel may reach another device: no remote copies, remote signals or barrier semaphores. Data moves between devices by JAX's collectives and lax.ppermute only.
A program may use at most 64 MiB of HBM per device.

v0:
```python
import math
import jax
import jax.numpy as jnp
from jax import lax
from jax.sharding import PartitionSpec as P

HD = 128
SPANS = 2
NEG_FILL = -1e30
EPSILON = 1e-06


def partial_attention(query_block, query_pos, cache_keys, cache_values, key_pos):
    rows_here = query_block.shape[0]
    kv_local = cache_keys.shape[1] // HD
    group_size = query_block.shape[1] // (kv_local * HD)
    heads_here = kv_local * group_size
    shaped_q = query_block.reshape(rows_here, kv_local, group_size, HD)
    shaped_k = cache_keys.reshape(-1, kv_local, HD)
    shaped_v = cache_values.reshape(-1, kv_local, HD)
    scores = jnp.einsum(
        "qgjd,kgd->qgjk", shaped_q, shaped_k, preferred_element_type=jnp.float32
    ) * (1.0 / math.sqrt(HD))
    visible = (key_pos[None, :] <= query_pos[:, None])[:, None, None, :]
    scores = jnp.where(visible, scores, NEG_FILL)
    row_top = jnp.max(scores, axis=-1)
    weights = jnp.where(visible, jnp.exp(scores - row_top[..., None]), 0.0)
    totals = jnp.sum(weights, axis=-1)
    numerator = jnp.einsum(
        "qgjk,kgd->qgjd", weights.astype(jnp.bfloat16), shaped_v, preferred_element_type=jnp.float32
    )
    return (
        row_top.reshape(rows_here, heads_here),
        totals.reshape(rows_here, heads_here),
        numerator.reshape(rows_here, heads_here * HD),
    )


def run_experts(arrived, gate_weight, up_weight, down_weight):
    gate_part = jnp.einsum(
        "secd,edf->secf", arrived, gate_weight, preferred_element_type=jnp.float32
    )
    up_part = jnp.einsum("secd,edf->secf", arrived, up_weight, preferred_element_type=jnp.float32)
    hidden = (jax.nn.silu(gate_part) * up_part).astype(jnp.bfloat16)
    return jnp.einsum(
        "secf,efd->secd", hidden, down_weight, preferred_element_type=jnp.float32
    ).astype(jnp.bfloat16)


def on_device(
    queries,
    cache_keys,
    cache_values,
    span_starts,
    out_weight,
    norm_gain,
    expert_ids,
    gate_fixed,
    gate_weight,
    up_weight,
    down_weight,
):
    gathered = lax.all_gather(queries, "blk", axis=0, tiled=True)
    total_rows = gathered.shape[0]
    width = gathered.shape[1]
    span_length = total_rows // SPANS
    token_index = jnp.arange(total_rows, dtype=jnp.int32)
    span_index = token_index // span_length
    span_match = span_index[:, None] == jnp.arange(SPANS, dtype=jnp.int32)[None, :]
    start_of = jnp.sum(jnp.where(span_match, span_starts[None, :], 0), axis=1)
    query_pos = start_of + token_index % span_length
    cache_rows = cache_keys.shape[0]
    key_pos = lax.axis_index("blk") * cache_rows + jnp.arange(cache_rows, dtype=jnp.int32)
    block_rows = math.gcd(total_rows, 128)
    block_count = total_rows // block_rows

    def one_block(item):
        return partial_attention(item[0], item[1], cache_keys, cache_values, key_pos)

    blocked = (
        gathered.reshape(block_count, block_rows, width),
        query_pos.reshape(block_count, block_rows),
    )
    row_top, totals, numerator = lax.map(one_block, blocked)
    heads_here = row_top.shape[2]
    row_top = row_top.reshape(total_rows, heads_here)
    totals = totals.reshape(total_rows, heads_here)
    numerator = numerator.reshape(total_rows, heads_here * HD)
    global_top = lax.pmax(row_top, "blk")
    factor = jnp.exp(row_top - global_top)
    totals = totals * factor
    numerator = (numerator.reshape(total_rows, heads_here, HD) * factor[:, :, None]).reshape(
        total_rows, heads_here * HD
    )
    own_numer = lax.psum_scatter(
        numerator.astype(jnp.bfloat16), "blk", scatter_dimension=1, tiled=True
    ).astype(jnp.float32)
    all_totals = lax.psum(totals, "blk")
    col_width = own_numer.shape[1]
    first_col = lax.axis_index("blk") * col_width
    spread = jnp.repeat(all_totals, HD, axis=1)
    col_totals = lax.dynamic_slice_in_dim(spread, first_col, col_width, 1)
    attended = (own_numer / col_totals).astype(jnp.bfloat16)
    projected = lax.psum_scatter(
        jnp.dot(attended, out_weight, preferred_element_type=jnp.float32),
        ("blk", "rows"),
        scatter_dimension=0,
        tiled=True,
    )
    attn_proj = projected.astype(jnp.bfloat16)
    values_f = attn_proj.astype(jnp.float32)
    mean_square = jnp.mean(values_f * values_f, axis=-1, keepdims=True)
    normed = (values_f * lax.rsqrt(mean_square + EPSILON) * norm_gain.astype(jnp.float32)).astype(
        jnp.bfloat16
    )
    own_tokens = normed.shape[0]
    top_count = expert_ids.shape[1]
    owners = lax.axis_size("blk") * lax.axis_size("rows")
    local_experts = gate_weight.shape[0]
    expert_count = owners * local_experts
    capacity = min(own_tokens, max(2, 2 * top_count * own_tokens // expert_count))
    slot_total = expert_count * capacity
    route_expert = expert_ids.reshape(-1)
    route_count = route_expert.shape[0]
    hits = (route_expert[:, None] == jnp.arange(expert_count, dtype=jnp.int32)[None, :]).astype(
        jnp.int32
    )
    slot_number = jnp.sum(jnp.cumsum(hits, axis=0) * hits, axis=1) - 1
    target = route_expert * capacity + slot_number
    placed = target[:, None] == jnp.arange(slot_total, dtype=jnp.int32)[None, :]
    route_token = jnp.arange(route_count, dtype=jnp.int32) // top_count
    token_pick = route_token[:, None] == jnp.arange(own_tokens, dtype=jnp.int32)[None, :]
    slot_token = jnp.dot(
        placed.astype(jnp.bfloat16).T,
        token_pick.astype(jnp.bfloat16),
        preferred_element_type=jnp.float32,
    ).astype(jnp.bfloat16)
    outgoing = jnp.dot(slot_token, normed, preferred_element_type=jnp.float32).astype(jnp.bfloat16)
    outgoing = outgoing.reshape(owners, local_experts, capacity, -1)
    gate_values = gate_fixed.astype(jnp.float32)
    route_weight = (gate_values / jnp.sum(gate_values, axis=1, keepdims=True)).reshape(-1)
    weighted_pick = token_pick.astype(jnp.float32) * route_weight[:, None]
    blend = jnp.dot(weighted_pick.T, placed.astype(jnp.float32), precision=lax.Precision.HIGHEST)
    finished = run_experts(
        lax.all_to_all(outgoing, ("blk", "rows"), split_axis=0, concat_axis=0, tiled=True),
        gate_weight,
        up_weight,
        down_weight,
    )
    returned = lax.all_to_all(finished, ("blk", "rows"), split_axis=0, concat_axis=0, tiled=True)
    returned_flat = returned.reshape(slot_total, -1)
    mixed = jnp.dot(blend, returned_flat.astype(jnp.float32), precision=lax.Precision.HIGHEST)
    expert_out = mixed.astype(jnp.bfloat16)
    return (attn_proj, expert_out)


def solution(mesh):
    in_specs = (
        P(("groups", "blk"), "rows"),
        P(("groups", "blk"), "rows"),
        P(("groups", "blk"), "rows"),
        P("groups"),
        P(("rows", "blk"), None),
        P(),
        P(("groups", "blk", "rows"), None),
        P(("groups", "blk", "rows"), None),
        P(("blk", "rows"), None, None),
        P(("blk", "rows"), None, None),
        P(("blk", "rows"), None, None),
    )
    out_specs = (P(("groups", "blk", "rows"), None), P(("groups", "blk", "rows"), None))
    return jax.shard_map(
        on_device, mesh=mesh, in_specs=in_specs, out_specs=out_specs, check_vma=False
    )
```

profile of v0, /device:TPU:0, one launch (start us, length us, event | category | flops | bytes accessed | tf_op | source)
XLA Modules:
  0.0 248.1 jit_solution(16907521409882701303)
XLA Ops:
  7.2 0.0 copy-start
  7.2 0.0 reduce-scatter.3.cloned.1.call-start
  7.3 0.9 fusion.69
  8.2 34.8 %all_gather.3 = bf16[128,1024]{1,0:T(8,128)(2,1)} all-gather(bf16[16,1024]{1,0:T(8,128)(2,1)} %param.11), channel_id=1, replica_groups=mesh['groups'=2,'blk'=8,'rows'=2] {'blk'}, dimensions={0}, use_global_device_ids=true | all-gather | bytes 294912 | tf_op jit(solution)/shard_map/all_gather | solution.py:63
  42.9 1.1 copy.25
  44.0 0.1 broadcast_compare_fusion
  44.2 2.7 %fusion.13 = (f32[128,8]{0,1:T(8,128)S(1)}, f32[512,128,8]{1,0,2:T(8,128)}) fusion(pred[128,512]{0,1:T(8,128)(4,1)S(1)} %broadcast_compare_fusion, bf16[128,8,128]{0,2,1:T(8,128)(2,1)S(1)} %bitcast.116, bf16[512,128]{1,0:T(8,128)(2,1)} %param.12), kind=kOutput, calls=%fused_computation.13 | convolution fusion | flops 135789568 | bytes 2560000 | tf_op jit(solution)/shard_map/while/body/eval_jaxpr/qgjd,kgd->qgjk/dot_general | solution.py:21
  46.9 21.3 %pmax.7 = f32[128,8]{0,1:T(8,128)S(1)} all-reduce(f32[128,8]{0,1:T(8,128)S(1)} %get-tuple-element.24), channel_id=1, replica_groups=mesh['groups'=2,'blk'=8,'rows'=2] {'blk'}, use_global_device_ids=true, to_apply=%region_2.3 | all-reduce | flops 1024 | bytes 8192 | tf_op jit(solution)/shard_map/pmax | solution.py:89
  68.2 0.0 copy-start.1
  68.2 2.2 fusion.14
  70.5 0.0 copy-done.1
  70.5 1.5 fusion.32
  72.0 0.0 copy-start.6
  72.0 0.0 copy-start.5
  72.1 0.7 fusion.37
  72.8 0.0 reduce-scatter.3.cloned.1.call-update
  72.8 0.0 reduce-scatter.5.cloned.1.call-start
  72.9 17.1 %psum.7 = f32[128,8]{0,1:T(8,128)S(1)} all-reduce(f32[128,8]{0,1:T(8,128)S(1)} %get-tuple-element.22), channel_id=1, replica_groups=mesh['groups'=2,'blk'=8,'rows'=2] {'blk'}, use_global_device_ids=true, to_apply=%region_5.6 | all-reduce | flops 1024 | bytes 8192 | tf_op jit(solution)/shard_map/psum | solution.py:98
  90.0 42.7 %reduce-scatter.3.cloned.1.call-done = bf16[128,128]{0,1:T(8,128)(2,1)} async-done(((bf16[128,1024]{0,1:T(8,128)(2,1)}), bf16[128,128]{0,1:T(8,128)(2,1)}) %reduce-scatter.3.cloned.1.call-update) | async-done | bytes 32784 | tf_op jit(solution)/shard_map/reduce_scatter | solution.py:95
  132.7 2.4 fusion.54
  135.1 0.0 reduce-scatter.5.cloned.1.call-update
  135.1 0.0 copy-done.6
  135.1 0.1 reshape.171
  135.2 0.1 fusion.59
  135.3 0.1 reduce_window_sum.11
  135.4 0.0 copy-done.5
  135.4 0.2 select_reduce_fusion
  135.6 57.3 %reduce-scatter.5.cloned.1.call-done = f32[8,2048]{1,0:T(8,128)} async-done(((f32[128,2048]{1,0:T(8,128)}), f32[8,2048]{1,0:T(8,128)}) %reduce-scatter.5.cloned.1.call-update) | async-done | bytes 65552 | tf_op jit(solution)/shard_map/reduce_scatter | solution.py:104
  192.9 1.0 fusion.51
  193.9 0.0 copy-start.3
  193.9 1.4 fusion.12
  195.3 0.0 copy-done.3
  195.3 18.0 %all_to_all.10 = bf16[16,1,8,2048]{3,2,1,0:T(8,128)(2,1)S(1)} all-to-all(bf16[16,1,8,2048]{3,2,1,0:T(8,128)(2,1)} %fusion.12), channel_id=1, replica_groups=mesh['groups'=2,'blk'=8,'rows'=2] {'blk','rows'}, dimensions={0} | all-to-all | bytes 1048576 | tf_op jit(solution)/shard_map/all_to_all | solution.py:145
  213.3 0.0 copy-start.2
  213.3 0.8 copy-done.2
  214.2 2.5 fusion.16
  216.6 0.0 copy-done
  216.6 0.0 copy-start.4
  216.7 4.1 %fusion.9 = bf16[16,1,8,2048]{3,2,1,0:T(8,128)(2,1)} fusion(bf16[1,768,2048]{2,1,0:T(8,128)(2,1)S(1)} %copy-done, bf16[1,2048,768]{2,1,0:T(8,128)(2,1)} %param.20, bf16[16,1,8,2048]{3,2,1,0:T(8,128)(2,1)} %copy-done.2, f32[16,1,8,768]{3,2,0,1:T(8,128)S(1)} %fusion.16), kind=kOutput, calls=%fused_computation.8 | convolution fusion | flops 806158336 | bytes 7733248 | tf_op jit(solution)/shard_map/secf,efd->secd/dot_general | solution.py:45
  220.7 4.2 %all-to-all-start.1 = ((bf16[16,1,8,2048]{3,2,1,0:T(8,128)(2,1)}), bf16[16,1,8,2048]{3,2,1,0:T(8,128)(2,1)}, u32[]{:S(2)}, u32[]{:S(2)}) async-start(bf16[16,1,8,2048]{3,2,1,0:T(8,128)(2,1)} %fusion.9), calls=%async_computation.3 | async-start | bytes 1048576 | tf_op jit(solution)/shard_map/all_to_all | solution.py:150
  225.0 0.0 copy-done.4
  225.0 0.1 convert_reduce_fusion
  225.1 0.1 convert_divide_fusion
  225.2 0.1 mul.86
  225.3 0.3 fusion.58
  225.5 13.8 %all-to-all-done.1 = bf16[16,1,8,2048]{3,2,1,0:T(8,128)(2,1)} async-done(((bf16[16,1,8,2048]{3,2,1,0:T(8,128)(2,1)}), bf16[16,1,8,2048]{3,2,1,0:T(8,128)(2,1)}, u32[]{:S(2)}, u32[]{:S(2)}) %all-to-all-start.1) | async-done | bytes 524320 | tf_op jit(solution)/shard_map/all_to_all | solution.py:150
  239.3 2.0 convolution_convert_fusion.1
  (8 shorter events, 0.1 us)
Async XLA Ops:
  7.2 209.5 %copy-start = (bf16[1,768,2048]{2,1,0:T(8,128)(2,1)S(1)}, bf16[1,768,2048]{2,1,0:T(8,128)(2,1)}, u32[]{:S(2)}) copy-start(bf16[1,768,2048]{2,1,0:T(8,128)(2,1)} %param.21) | copy-start | bytes 9437188
  7.2 125.5 %reduce-scatter.3.cloned.1.call-start = ((), (), s32[]{:S(2)}) async-start(), calls=%async_computation.4 | async-start | bytes 294912 | tf_op jit(solution)/shard_map/reduce_scatter | solution.py:95
  68.2 2.3 copy-start.1
  72.0 63.1 %copy-start.6 = (s32[8,8]{1,0:T(8,128)S(1)}, s32[8,8]{1,0:T(8,128)}, u32[]{:S(2)}) copy-start(s32[8,8]{1,0:T(8,128)} %param.17) | copy-start | bytes 772
  72.0 63.4 %copy-start.5 = (bf16[2048]{0:T(1024)(128)(2,1)S(1)}, bf16[2048]{0:T(1024)(128)(2,1)}, u32[]{:S(2)}) copy-start(bf16[2048]{0:T(1024)(128)(2,1)} %param.16) | copy-start | bytes 12292
  72.8 120.1 %reduce-scatter.5.cloned.1.call-start = ((), (), s32[]{:S(2)}) async-start(), calls=%async_computation.5 | async-start | bytes 1114112 | tf_op jit(solution)/shard_map/reduce_scatter | solution.py:104
  193.9 1.4 copy-start.3
  213.3 0.8 copy-start.2
  216.6 8.3 %copy-start.4 = (s32[8,8]{1,0:T(8,128)S(1)}, s32[8,8]{1,0:T(8,128)}, u32[]{:S(2)}) copy-start(s32[8,8]{1,0:T(8,128)} %param.18) | copy-start | bytes 772
  220.7 18.6 %all-to-all-start.1 = ((bf16[16,1,8,2048]{3,2,1,0:T(8,128)(2,1)}), bf16[16,1,8,2048]{3,2,1,0:T(8,128)(2,1)}, u32[]{:S(2)}, u32[]{:S(2)}) async-start(bf16[16,1,8,2048]{3,2,1,0:T(8,128)(2,1)} %fusion.9), calls=%async_computation.3 | async-start | bytes 1048576 | tf_op jit(solution)/shard_map/all_to_all | solution.py:150
Sparse Core Ops, SparseCore 0:
  72.9 59.7 reduce-scatter.2
  136.3 56.6 reduce-scatter.4
where the time goes:
time: 249 us; the launch traced here: 248 us
  waiting for transfers between devices  114 us (46%)
  blocking collectives  91.3 us (37%)
  matrix products  16.8 us (7%)
  between operations  14.2 us (6%)
  other arithmetic  5.54 us (2%)
  starting transfers between devices  4.32 us (2%)
    reduce_scatter x1, waiting for transfers between devices, on_device(): lax.psum_scatter(jnp.dot(attended, out_weight, preferred_element_type=jnp...  57.3 us
    reduce_scatter x1, waiting for transfers between devices, on_device(): lax.psum_scatter(numerator.astype(jnp.bfloat16), 'blk', scatter_dimension...  42.7 us
    all_gather x1, blocking collectives, on_device(): gathered = lax.all_gather(queries, 'blk', axis=0, tiled=True)  34.8 us
    pmax x1, blocking collectives, on_device(): global_top = lax.pmax(row_top, 'blk')  21.3 us
    all_to_all x1, blocking collectives, on_device(): lax.all_to_all(outgoing, ('blk', 'rows'), split_axis=0, concat_axis=0, ti...  18 us
    psum x1, blocking collectives, on_device(): all_totals = lax.psum(totals, 'blk')  17.1 us
    all_to_all x1, waiting for transfers between devices, on_device(): lax.all_to_all(finished, ('blk', 'rows'), split_axis=0, concat_axis=0, ti...  13.8 us
  transfers between devices with their start and end apart: 3, of which 3 were waited for; matrix products, arithmetic and copies ran while one was open for 0% of the time, Pallas kernels for 0%

commit v1 on v0

--- a/solution.py
+++ b/solution.py
@@ -60,7 +60,16 @@
     up_weight,
     down_weight,
 ):
-    gathered = lax.all_gather(queries, "blk", axis=0, tiled=True)
+    detail_the_corner = lambda vector, axis_tag: jnp.concatenate(
+        jax.lax.all_to_all(
+            jnp.stack([vector for _ in range(jax.lax.axis_size(axis_tag))]),
+            axis_name=axis_tag,
+            split_axis=0,
+            concat_axis=0,
+        ),
+        0,
+    )
+    gathered = detail_the_corner(queries, axis_tag="blk")
     total_rows = gathered.shape[0]
     width = gathered.shape[1]
     span_length = total_rows // SPANS

time: 249 us -> 227 us (0.912)
  blocking collectives: 91.3 us -> 54.6 us
  waiting for transfers between devices: 114 us -> 122 us
  starting transfers between devices: 4.32 us -> 11.6 us
    all_gather x1 -> x0, blocking collectives: 34.8 us -> none  [on_device(): gathered = lax.all_gather(queries, 'blk', axis=0, tiled=True)]
    all_to_all x0 -> x1, waiting for transfers between devices: none -> 7.96 us  [on_device(): jax.lax.all_to_all(jnp.stack([vector for _ in range(jax.lax.axis_size(axi...]
    all_to_all x0 -> x1, starting transfers between devices: none -> 7.31 us  [on_device(): jax.lax.all_to_all(jnp.stack([vector for _ in range(jax.lax.axis_size(axi...]
  transfers between devices with their start and end apart: 3 -> 4, of which waited for: 3 -> 4; matrix products, arithmetic and copies ran while one was open for 0% -> 1% of each run, Pallas kernels for 0% -> 0%
where the time goes in v1:
time: 227 us; the launch traced here: 226 us
  waiting for transfers between devices  122 us (54%)
  blocking collectives  54.6 us (24%)
  matrix products  15.9 us (7%)
  between operations  14.2 us (6%)
  starting transfers between devices  11.6 us (5%)
  other arithmetic  5.38 us (2%)
  local copies, waits for them, and re-layouts  2.72 us (1%)
    reduce_scatter x1, waiting for transfers between devices, on_device(): lax.psum_scatter(jnp.dot(attended, out_weight, preferred_element_type=jnp...  57.4 us
    reduce_scatter x1, waiting for transfers between devices, on_device(): lax.psum_scatter(numerator.astype(jnp.bfloat16), 'blk', scatter_dimension...  42.7 us
    pmax x1, blocking collectives, on_device(): global_top = lax.pmax(row_top, 'blk')  19.4 us
    all_to_all x1, blocking collectives, on_device(): lax.all_to_all(outgoing, ('blk', 'rows'), split_axis=0, concat_axis=0, ti...  18.1 us
    psum x1, blocking collectives, on_device(): all_totals = lax.psum(totals, 'blk')  17.1 us
    all_to_all x1, waiting for transfers between devices, on_device(): lax.all_to_all(finished, ('blk', 'rows'), split_axis=0, concat_axis=0, ti...  13.8 us
    all_to_all x1, waiting for transfers between devices, on_device(): jax.lax.all_to_all(jnp.stack([vector for _ in range(jax.lax.axis_size(axi...  7.96 us
    all_to_all x1, starting transfers between devices, on_device(): jax.lax.all_to_all(jnp.stack([vector for _ in range(jax.lax.axis_size(axi...  7.31 us
  transfers between devices with their start and end apart: 4, of which 4 were waited for; matrix products, arithmetic and copies ran while one was open for 1% of the time, Pallas kernels for 0%

profile of v1, /device:TPU:0, one launch (start us, length us, event | category | flops | bytes accessed | tf_op | source)
XLA Modules:
  0.0 226.3 jit_solution(11438854006227389007)
XLA Ops:
  7.2 0.0 copy-start
  7.2 1.6 stack.2
  8.8 7.3 %all-to-all-start = ((bf16[8,16,1024]{2,1,0:T(8,128)(2,1)}), bf16[8,16,1024]{2,1,0:T(8,128)(2,1)S(1)}, u32[]{:S(2)}, u32[]{:S(2)}) async-start(bf16[8,16,1024]{2,1,0:T(8,128)(2,1)} %stack.2), calls=%async_computation | async-start | bytes 524288 | tf_op jit(solution)/shard_map/all_to_all | solution.py:64
  16.1 0.0 reduce-scatter.3.cloned.1.call-start
  16.2 0.7 fusion.70
  16.9 0.1 broadcast_compare_fusion
  17.1 8.0 %all-to-all-done = bf16[8,16,1024]{2,1,0:T(8,128)(2,1)S(1)} async-done(((bf16[8,16,1024]{2,1,0:T(8,128)(2,1)}), bf16[8,16,1024]{2,1,0:T(8,128)(2,1)S(1)}, u32[]{:S(2)}, u32[]{:S(2)}) %all-to-all-start) | async-done | bytes 262176 | tf_op jit(solution)/shard_map/all_to_all | solution.py:64
  25.1 0.0 copy-start.7
  25.1 2.7 %fusion.13 = (f32[128,8]{0,1:T(8,128)S(1)}, f32[512,128,8]{1,0,2:T(8,128)}) fusion(pred[128,512]{0,1:T(8,128)(4,1)S(1)} %broadcast_compare_fusion, bf16[128,8,128]{2,1,0:T(8,128)(2,1)S(1)} %bitcast.117, bf16[512,128]{1,0:T(8,128)(2,1)} %param.12), kind=kOutput, calls=%fused_computation.13 | convolution fusion | flops 135789568 | bytes 2560000 | tf_op jit(solution)/shard_map/while/body/eval_jaxpr/qgjd,kgd->qgjk/dot_general | solution.py:21
  27.8 19.4 %pmax.7 = f32[128,8]{0,1:T(8,128)S(1)} all-reduce(f32[128,8]{0,1:T(8,128)S(1)} %get-tuple-element.24), channel_id=1, replica_groups=mesh['groups'=2,'blk'=8,'rows'=2] {'blk'}, use_global_device_ids=true, to_apply=%region_2.3 | all-reduce | flops 1024 | bytes 8192 | tf_op jit(solution)/shard_map/pmax | solution.py:98
  47.2 0.0 copy-start.1
  47.2 2.2 fusion.14
  49.5 0.0 copy-done.7
  49.5 0.0 copy-done.1
  49.5 0.6 fusion.32
  50.2 0.0 copy-start.6
  50.2 0.0 copy-start.5
  50.2 0.7 fusion.37
  50.9 0.0 reduce-scatter.3.cloned.1.call-update
  50.9 0.0 reduce-scatter.5.cloned.1.call-start
  51.0 17.1 %psum.7 = f32[128,8]{0,1:T(8,128)S(1)} all-reduce(f32[128,8]{0,1:T(8,128)S(1)} %get-tuple-element.22), channel_id=1, replica_groups=mesh['groups'=2,'blk'=8,'rows'=2] {'blk'}, use_global_device_ids=true, to_apply=%region_5.6 | all-reduce | flops 1024 | bytes 8192 | tf_op jit(solution)/shard_map/psum | solution.py:107
  68.1 42.7 %reduce-scatter.3.cloned.1.call-done = bf16[128,128]{0,1:T(8,128)(2,1)} async-done(((bf16[128,1024]{0,1:T(8,128)(2,1)}), bf16[128,128]{0,1:T(8,128)(2,1)}) %reduce-scatter.3.cloned.1.call-update) | async-done | bytes 32784 | tf_op jit(solution)/shard_map/reduce_scatter | solution.py:104
  110.9 2.4 %fusion.55 = f32[128,2048]{1,0:T(8,128)} fusion(bf16[128,2048]{1,0:T(8,128)(2,1)} %param.15, f32[128,1024]{0,1:T(8,128)S(1)} %bitcast.119, s32[]{:T(128)S(6)} %select_n.48, bf16[128,128]{0,1:T(8,128)(2,1)} %reduce-scatter.3.cloned.1.call-done), kind=kOutput, calls=%fused_computation.47 | convolution fusion | flops 67158016 | bytes 1671172 | tf_op jit(solution)/shard_map/dot_general | solution.py:114
  113.3 0.0 reduce-scatter.5.cloned.1.call-update
  113.3 0.0 copy-done.6
  113.3 0.1 reshape.171
  113.4 0.1 fusion.60
  113.4 0.1 reduce_window_sum.11
  113.5 0.0 copy-done.5
  113.6 0.2 select_reduce_fusion
  113.7 57.4 %reduce-scatter.5.cloned.1.call-done = f32[8,2048]{1,0:T(8,128)} async-done(((f32[128,2048]{1,0:T(8,128)}), f32[8,2048]{1,0:T(8,128)}) %reduce-scatter.5.cloned.1.call-update) | async-done | bytes 65552 | tf_op jit(solution)/shard_map/reduce_scatter | solution.py:113
  171.1 1.0 fusion.52
  172.1 1.4 fusion.12
  173.5 0.0 copy-done.3
  173.5 18.1 %all_to_all.15 = bf16[16,1,8,2048]{3,2,1,0:T(8,128)(2,1)S(1)} all-to-all(bf16[16,1,8,2048]{3,2,1,0:T(8,128)(2,1)} %fusion.12), channel_id=1, replica_groups=mesh['groups'=2,'blk'=8,'rows'=2] {'blk','rows'}, dimensions={0} | all-to-all | bytes 1048576 | tf_op jit(solution)/shard_map/all_to_all | solution.py:154
  191.6 0.8 copy-done.2
  192.4 2.5 %fusion.16 = f32[16,1,8,768]{3,2,0,1:T(8,128)S(1)} fusion(bf16[1,2048,768]{2,1,0:T(8,128)(2,1)} %param.19, bf16[16,1,8,2048]{3,2,1,0:T(8,128)(2,1)S(1)} %all_to_all.15), kind=kOutput, calls=%fused_computation.16 | convolution fusion | flops 402653184 | bytes 4063232 | tf_op jit(solution)/shard_map/secd,edf->secf/dot_general | solution.py:40
  194.8 0.0 copy-done
  194.9 0.0 copy-start.4
  194.9 4.1 %fusion.9 = bf16[16,1,8,2048]{3,2,1,0:T(8,128)(2,1)} fusion(bf16[1,768,2048]{2,1,0:T(8,128)(2,1)S(1)} %copy-done, bf16[1,2048,768]{2,1,0:T(8,128)(2,1)} %param.20, bf16[16,1,8,2048]{3,2,1,0:T(8,128)(2,1)} %copy-done.2, f32[16,1,8,768]{3,2,0,1:T(8,128)S(1)} %fusion.16), kind=kOutput, calls=%fused_computation.8 | convolution fusion | flops 806158336 | bytes 7733248 | tf_op jit(solution)/shard_map/secf,efd->secd/dot_general | solution.py:45
  198.9 4.2 %all-to-all-start.2 = ((bf16[16,1,8,2048]{3,2,1,0:T(8,128)(2,1)}), bf16[16,1,8,2048]{3,2,1,0:T(8,128)(2,1)}, u32[]{:S(2)}, u32[]{:S(2)}) async-start(bf16[16,1,8,2048]{3,2,1,0:T(8,128)(2,1)} %fusion.9), calls=%async_computation.4 | async-start | bytes 1048576 | tf_op jit(solution)/shard_map/all_to_all | solution.py:159
  203.2 0.0 copy-done.4
  203.2 0.1 convert_reduce_fusion
  203.3 0.1 convert_divide_fusion
  203.4 0.1 mul.86
  203.5 0.3 fusion.59
  203.8 13.8 %all-to-all-done.2 = bf16[16,1,8,2048]{3,2,1,0:T(8,128)(2,1)} async-done(((bf16[16,1,8,2048]{3,2,1,0:T(8,128)(2,1)}), bf16[16,1,8,2048]{3,2,1,0:T(8,128)(2,1)}, u32[]{:S(2)}, u32[]{:S(2)}) %all-to-all-start.2) | async-done | bytes 524320 | tf_op jit(solution)/shard_map/all_to_all | solution.py:159
  217.5 2.0 convolution_convert_fusion.1
  (11 shorter events, 0.1 us)
Async XLA Ops:
  7.2 187.7 %copy-start = (bf16[1,768,2048]{2,1,0:T(8,128)(2,1)S(1)}, bf16[1,768,2048]{2,1,0:T(8,128)(2,1)}, u32[]{:S(2)}) copy-start(bf16[1,768,2048]{2,1,0:T(8,128)(2,1)} %param.21) | copy-start | bytes 9437188
  8.8 16.2 %all-to-all-start = ((bf16[8,16,1024]{2,1,0:T(8,128)(2,1)}), bf16[8,16,1024]{2,1,0:T(8,128)(2,1)S(1)}, u32[]{:S(2)}, u32[]{:S(2)}) async-start(bf16[8,16,1024]{2,1,0:T(8,128)(2,1)} %stack.2), calls=%async_computation | async-start | bytes 524288 | tf_op jit(solution)/shard_map/all_to_all | solution.py:64
  16.1 94.7 %reduce-scatter.3.cloned.1.call-start = ((), (), s32[]{:S(2)}) async-start(), calls=%async_computation.5 | async-start | bytes 294912 | tf_op jit(solution)/shard_map/reduce_scatter | solution.py:104
  25.1 24.4 %copy-start.7 = (bf16[512,128]{1,0:T(8,128)(2,1)S(1)}, bf16[512,128]{1,0:T(8,128)(2,1)}, u32[]{:S(2)}) copy-start(bf16[512,128]{1,0:T(8,128)(2,1)} %param.13) | copy-start | bytes 393220
  47.2 2.3 copy-start.1
  50.2 63.1 %copy-start.6 = (s32[8,8]{1,0:T(8,128)S(1)}, s32[8,8]{1,0:T(8,128)}, u32[]{:S(2)}) copy-start(s32[8,8]{1,0:T(8,128)} %param.17) | copy-start | bytes 772
  50.2 63.4 %copy-start.5 = (bf16[2048]{0:T(1024)(128)(2,1)S(1)}, bf16[2048]{0:T(1024)(128)(2,1)}, u32[]{:S(2)}) copy-start(bf16[2048]{0:T(1024)(128)(2,1)} %param.16) | copy-start | bytes 12292
  50.9 120.2 %reduce-scatter.5.cloned.1.call-start = ((), (), s32[]{:S(2)}) async-start(), calls=%async_computation.6 | async-start | bytes 1114112 | tf_op jit(solution)/shard_map/reduce_scatter | solution.py:113
  172.1 1.4 copy-start.3
  191.6 0.8 copy-start.2
  194.9 8.3 %copy-start.4 = (s32[8,8]{1,0:T(8,128)S(1)}, s32[8,8]{1,0:T(8,128)}, u32[]{:S(2)}) copy-start(s32[8,8]{1,0:T(8,128)} %param.18) | copy-start | bytes 772
  198.9 18.6 %all-to-all-start.2 = ((bf16[16,1,8,2048]{3,2,1,0:T(8,128)(2,1)}), bf16[16,1,8,2048]{3,2,1,0:T(8,128)(2,1)}, u32[]{:S(2)}, u32[]{:S(2)}) async-start(bf16[16,1,8,2048]{3,2,1,0:T(8,128)(2,1)} %fusion.9), calls=%async_computation.4 | async-start | bytes 1048576 | tf_op jit(solution)/shard_map/all_to_all | solution.py:159
Sparse Core Ops, SparseCore 0:
  51.1 59.7 reduce-scatter.2
  114.4 56.6 reduce-scatter.4
